TPU v7x, 32 devices: a whole 2x2x4 slice. The times are simulated.
32 devices in a mesh: dp: 8 (over z, y), seq: 4 (over x, core).
Axes of the slice: x: 2, y: 2, z: 4, core: 2. Of those that a mesh axis runs over, the one named last changes fastest.
Arguments:
- tokens: bfloat16 [16, 1024, 768], P('dp', 'seq'), may hold values from -6 to 6
- lengths: int32 [16], P('dp'), may hold values from 128 to 1024, as said below
- entry_gain: bfloat16 [768], P(('dp', 'seq')), may hold values from 0.5 to 1.5
- entry_shift: bfloat16 [768], P(('dp', 'seq')), may hold values from -1 to 1
- joined_weight: bfloat16 [768, 2304], P(('dp', 'seq')), may hold values from -0.3125 to 0.3125
- joined_bias: bfloat16 [1536], P(('dp', 'seq')), may hold values from -1 to 1
- mixer_weight: bfloat16 [768, 768], P(('dp', 'seq')), may hold values from -1.25 to 1.25
- mixer_bias: bfloat16 [768], P(('dp', 'seq')), may hold values from -1 to 1
- middle_gain: bfloat16 [768], P(('dp', 'seq')), may hold values from 0.5 to 1.5
- middle_shift: bfloat16 [768], P(('dp', 'seq')), may hold values from -1 to 1
- widen_weight: bfloat16 [768, 3072], P(('dp', 'seq')), may hold values from -0.21875 to 0.21875
- widen_bias: bfloat16 [3072], P(('dp', 'seq')), may hold values from -1 to 1
- narrow_weight: bfloat16 [3072, 768], P(('dp', 'seq')), may hold values from -0.109375 to 0.109375
- narrow_bias: bfloat16 [768], P(('dp', 'seq')), may hold values from -1 to 1
- cotangent: bfloat16 [16, 1024, 768], P('dp', 'seq'), may hold values from -6 to 6
Outputs:
- mixed_out: bfloat16 [16, 1024, 768], P('dp', 'seq')
- tokens_grad: bfloat16 [16, 1024, 768], P('dp', 'seq')
- entry_gain_grad: float32 [768], P(('dp', 'seq'))
- entry_shift_grad: float32 [768], P(('dp', 'seq'))
- joined_weight_grad: float32 [768, 2304], P(('dp', 'seq'))
- joined_bias_grad: float32 [1536], P(('dp', 'seq'))
- mixer_weight_grad: float32 [768, 768], P(('dp', 'seq'))
- mixer_bias_grad: float32 [768], P(('dp', 'seq'))
- middle_gain_grad: float32 [768], P(('dp', 'seq'))
- middle_shift_grad: float32 [768], P(('dp', 'seq'))
- widen_weight_grad: float32 [768, 3072], P(('dp', 'seq'))
- widen_bias_grad: float32 [3072], P(('dp', 'seq'))
- narrow_weight_grad: float32 [3072, 768], P(('dp', 'seq'))
- narrow_bias_grad: float32 [768], P(('dp', 'seq'))
Inputs may be any that keep to these rules, and one draw needn't show every extreme that they name: `lengths`: some sequence holds all 1024 slots as true tokens.
All inputs are finite; a program needn't handle non-finite values.
Results may differ from a plain program's by a relative error of at most 0.024.
The roundings to bfloat16 on the way count: a program that leaves them out, or rounds other values in their place, can miss the bound.
Values may be sent and summed in bfloat16 or wider, within the bound.
No kernel may reach another device: no remote copies, remote signals or barrier semaphores. Data moves between devices by JAX's collectives and lax.ppermute only.
A program may use at most 192 MiB of HBM per device.

v0:
```python
import jax
import jax.numpy as jnp
from jax import lax
from jax.sharding import PartitionSpec as P

HD = 64
LAYERS = 2


EPSILON = 1e-05
NEGATIVE = -1e30
BLOCK_LIMIT = 512


def layer_norm(inputs, gain_row, shift_row):
    center = jnp.mean(inputs, axis=-1, keepdims=True)
    offset = inputs - center
    spread = jnp.mean(offset * offset, axis=-1, keepdims=True)
    return offset * lax.rsqrt(spread + EPSILON) * gain_row + shift_row


def gelu_tanh(values):
    return jax.nn.gelu(values, approximate=True)


def to_items(packed, heads_here):
    seq_count, total_rows, features = packed.shape
    head_size = features // heads_here
    return (
        packed.reshape(seq_count, total_rows, heads_here, head_size)
        .transpose(0, 2, 1, 3)
        .reshape(seq_count * heads_here, total_rows, head_size)
    )


def from_items(items, seq_count):
    item_count, total_rows, head_size = items.shape
    heads_here = item_count // seq_count
    return (
        items.reshape(seq_count, heads_here, total_rows, head_size)
        .transpose(0, 2, 1, 3)
        .reshape(seq_count, total_rows, heads_here * head_size)
    )


def block_mask(first_row, block_rows, length, total_rows):
    query_places = first_row + jnp.arange(block_rows, dtype=jnp.int32)[:, None]
    key_places = jnp.arange(total_rows, dtype=jnp.int32)[None, :]
    return (key_places <= query_places) & (key_places < length)


def attend_forward(packet):
    queries, key_rows, values, length = packet
    total_rows, head_size = queries.shape
    block_rows = min(BLOCK_LIMIT, total_rows)
    block_count = total_rows // block_rows
    scaling = head_size ** (-0.5)

    def one_block(portion):
        query_block, first_row = portion
        scores = (
            jnp.einsum("qd,kd->qk", query_block, key_rows, preferred_element_type=jnp.float32)
            * scaling
        )
        masked = jnp.where(block_mask(first_row, block_rows, length, total_rows), scores, NEGATIVE)
        row_top = jnp.max(masked, axis=1, keepdims=True)
        lifted = jnp.exp(masked - row_top)
        summed = jnp.sum(lifted, axis=1, keepdims=True)
        shares = (lifted / summed).astype(jnp.bfloat16)
        result = jnp.einsum("qk,kd->qd", shares, values, preferred_element_type=jnp.float32)
        return (result, (row_top + jnp.log(summed))[:, 0])

    starts = jnp.arange(block_count, dtype=jnp.int32) * block_rows
    results, logsum = lax.map(
        one_block, (queries.reshape(block_count, block_rows, head_size), starts)
    )
    return (results.reshape(total_rows, head_size), logsum.reshape(total_rows))


def attend_backward(packet):
    queries, key_rows, values, upstream, logsum, length = packet
    total_rows, head_size = queries.shape
    block_rows = min(BLOCK_LIMIT, total_rows)
    block_count = total_rows // block_rows
    scaling = head_size ** (-0.5)

    def one_block(running, portion):
        key_sum, value_sum = running
        query_block, upstream_block, logsum_block, first_row = portion
        scores = (
            jnp.einsum("qd,kd->qk", query_block, key_rows, preferred_element_type=jnp.float32)
            * scaling
        )
        shares = jnp.where(
            block_mask(first_row, block_rows, length, total_rows),
            jnp.exp(scores - logsum_block[:, None]),
            0.0,
        )
        value_sum = value_sum + jnp.einsum(
            "qk,qd->kd",
            shares.astype(jnp.bfloat16),
            upstream_block,
            preferred_element_type=jnp.float32,
        )
        share_grad = jnp.einsum(
            "qd,kd->qk", upstream_block, values, preferred_element_type=jnp.float32
        )
        centre = jnp.sum(share_grad * shares, axis=1, keepdims=True)
        score_grad = (shares * (share_grad - centre)).astype(jnp.bfloat16)
        query_grad = (
            jnp.einsum("qk,kd->qd", score_grad, key_rows, preferred_element_type=jnp.float32)
            * scaling
        )
        key_sum = (
            key_sum
            + jnp.einsum("qk,qd->kd", score_grad, query_block, preferred_element_type=jnp.float32)
            * scaling
        )
        return ((key_sum, value_sum), query_grad)

    zero_rows = jnp.zeros((total_rows, head_size), jnp.float32)
    starts = jnp.arange(block_count, dtype=jnp.int32) * block_rows
    (key_sum, value_sum), query_grads = lax.scan(
        one_block,
        (zero_rows, zero_rows),
        (
            queries.reshape(block_count, block_rows, head_size),
            upstream.reshape(block_count, block_rows, head_size),
            logsum.reshape(block_count, block_rows),
            starts,
        ),
    )
    return (
        query_grads.reshape(total_rows, head_size).astype(jnp.bfloat16),
        key_sum.astype(jnp.bfloat16),
        value_sum.astype(jnp.bfloat16),
    )


def forward_layer(stream, gathered, lengths, seq_count):
    (
        entry_gain,
        entry_shift,
        joined_weight,
        joined_bias,
        mixer_weight,
        mixer_bias,
        middle_gain,
        middle_shift,
        widen_weight,
        widen_bias,
        narrow_weight,
        narrow_bias,
    ) = gathered
    features = stream.shape[1]
    local_rows = stream.shape[0] // seq_count
    normed = layer_norm(
        stream, entry_gain.astype(jnp.float32), entry_shift.astype(jnp.float32)
    ).astype(jnp.bfloat16)
    bias_row = jnp.concatenate(
        [joined_bias[:features], jnp.zeros((features,), jnp.bfloat16), joined_bias[features:]]
    ).astype(jnp.float32)
    joined_rows = (
        jnp.dot(normed, joined_weight, preferred_element_type=jnp.float32) + bias_row
    ).astype(jnp.bfloat16)
    headed = lax.all_to_all(
        joined_rows.reshape(seq_count, local_rows, 3, features),
        "seq",
        split_axis=3,
        concat_axis=1,
        tiled=True,
    )
    heads_here = headed.shape[3] // HD
    queries = to_items(headed[:, :, 0], heads_here)
    key_rows = to_items(headed[:, :, 1], heads_here)
    values = to_items(headed[:, :, 2], heads_here)
    item_lengths = jnp.repeat(lengths, heads_here)
    mixed_rows, logsum = lax.map(attend_forward, (queries, key_rows, values, item_lengths))
    returned = lax.all_to_all(
        from_items(mixed_rows.astype(jnp.bfloat16), seq_count),
        "seq",
        split_axis=1,
        concat_axis=2,
        tiled=True,
    )
    attended = returned.reshape(seq_count * local_rows, features)
    middle = (
        stream
        + jnp.dot(attended, mixer_weight, preferred_element_type=jnp.float32)
        + mixer_bias.astype(jnp.float32)
    )
    normed_two = layer_norm(
        middle, middle_gain.astype(jnp.float32), middle_shift.astype(jnp.float32)
    ).astype(jnp.bfloat16)
    widened = jnp.dot(
        normed_two, widen_weight, preferred_element_type=jnp.float32
    ) + widen_bias.astype(jnp.float32)
    activated = gelu_tanh(widened).astype(jnp.bfloat16)
    output = (
        middle
        + jnp.dot(activated, narrow_weight, preferred_element_type=jnp.float32)
        + narrow_bias.astype(jnp.float32)
    )
    saved = (
        stream,
        normed,
        queries,
        key_rows,
        values,
        logsum,
        attended,
        middle,
        normed_two,
        widened,
        activated,
    )
    return (output, saved)


def backward_layer(upstream, saved, gathered, lengths, seq_count):
    (
        entry_gain,
        entry_shift,
        joined_weight,
        joined_bias,
        mixer_weight,
        mixer_bias,
        middle_gain,
        middle_shift,
        widen_weight,
        widen_bias,
        narrow_weight,
        narrow_bias,
    ) = gathered
    (
        stream,
        normed,
        queries,
        key_rows,
        values,
        logsum,
        attended,
        middle,
        normed_two,
        widened,
        activated,
    ) = saved
    features = stream.shape[1]
    local_rows = stream.shape[0] // seq_count
    branch_grad = upstream.astype(jnp.bfloat16)
    narrow_weight_term = jnp.einsum(
        "tf,td->fd", activated, branch_grad, preferred_element_type=jnp.float32
    )
    narrow_bias_term = jnp.sum(branch_grad.astype(jnp.float32), axis=0)
    activated_grad = jnp.einsum(
        "td,fd->tf", branch_grad, narrow_weight, preferred_element_type=jnp.float32
    )
    widened_grad = jax.vjp(gelu_tanh, widened)[1](activated_grad)[0].astype(jnp.bfloat16)
    widen_weight_term = jnp.einsum(
        "td,tf->df", normed_two, widened_grad, preferred_element_type=jnp.float32
    )
    widen_bias_term = jnp.sum(widened_grad.astype(jnp.float32), axis=0)
    normed_two_grad = jnp.einsum(
        "tf,df->td", widened_grad, widen_weight, preferred_element_type=jnp.float32
    )
    middle_pull = jax.vjp(
        layer_norm, middle, middle_gain.astype(jnp.float32), middle_shift.astype(jnp.float32)
    )[1]
    middle_grad, middle_gain_term, middle_shift_term = middle_pull(normed_two_grad)
    middle_grad = middle_grad + upstream
    mixer_grad = middle_grad.astype(jnp.bfloat16)
    mixer_weight_term = jnp.einsum(
        "te,td->ed", attended, mixer_grad, preferred_element_type=jnp.float32
    )
    mixer_bias_term = jnp.sum(mixer_grad.astype(jnp.float32), axis=0)
    attended_grad = jnp.einsum(
        "td,ed->te", mixer_grad, mixer_weight, preferred_element_type=jnp.float32
    ).astype(jnp.bfloat16)
    heads_grad = lax.all_to_all(
        attended_grad.reshape(seq_count, local_rows, features),
        "seq",
        split_axis=2,
        concat_axis=1,
        tiled=True,
    )
    heads_here = heads_grad.shape[2] // HD
    item_lengths = jnp.repeat(lengths, heads_here)
    query_grad, key_grad, value_grad = lax.map(
        attend_backward,
        (queries, key_rows, values, to_items(heads_grad, heads_here), logsum, item_lengths),
    )
    stacked = jnp.stack(
        [
            from_items(query_grad, seq_count),
            from_items(key_grad, seq_count),
            from_items(value_grad, seq_count),
        ],
        axis=2,
    )
    joined_grad = lax.all_to_all(stacked, "seq", split_axis=1, concat_axis=3, tiled=True).reshape(
        seq_count * local_rows, 3 * features
    )
    joined_weight_term = jnp.einsum(
        "td,te->de", normed, joined_grad, preferred_element_type=jnp.float32
    )
    joined_sums = jnp.sum(joined_grad.astype(jnp.float32), axis=0)
    joined_bias_term = jnp.concatenate([joined_sums[:features], joined_sums[2 * features :]])
    normed_grad = jnp.einsum(
        "te,de->td", joined_grad, joined_weight, preferred_element_type=jnp.float32
    )
    entry_pull = jax.vjp(
        layer_norm, stream, entry_gain.astype(jnp.float32), entry_shift.astype(jnp.float32)
    )[1]
    stream_grad, entry_gain_term, entry_shift_term = entry_pull(normed_grad)
    stream_grad = stream_grad + middle_grad
    grad_terms = (
        entry_gain_term,
        entry_shift_term,
        joined_weight_term,
        joined_bias_term,
        mixer_weight_term,
        mixer_bias_term,
        middle_gain_term,
        middle_shift_term,
        widen_weight_term,
        widen_bias_term,
        narrow_weight_term,
        narrow_bias_term,
    )
    return (stream_grad, grad_terms)


def local(
    tokens,
    lengths,
    entry_gain,
    entry_shift,
    joined_weight,
    joined_bias,
    mixer_weight,
    mixer_bias,
    middle_gain,
    middle_shift,
    widen_weight,
    widen_bias,
    narrow_weight,
    narrow_bias,
    cotangent,
):
    gathered = (
        lax.all_gather(entry_gain, ("dp", "seq"), axis=0, tiled=True),
        lax.all_gather(entry_shift, ("dp", "seq"), axis=0, tiled=True),
        lax.all_gather(joined_weight, ("dp", "seq"), axis=0, tiled=True),
        lax.all_gather(joined_bias, ("dp", "seq"), axis=0, tiled=True),
        lax.all_gather(mixer_weight, ("dp", "seq"), axis=0, tiled=True),
        lax.all_gather(mixer_bias, ("dp", "seq"), axis=0, tiled=True),
        lax.all_gather(middle_gain, ("dp", "seq"), axis=0, tiled=True),
        lax.all_gather(middle_shift, ("dp", "seq"), axis=0, tiled=True),
        lax.all_gather(widen_weight, ("dp", "seq"), axis=0, tiled=True),
        lax.all_gather(widen_bias, ("dp", "seq"), axis=0, tiled=True),
        lax.all_gather(narrow_weight, ("dp", "seq"), axis=0, tiled=True),
        lax.all_gather(narrow_bias, ("dp", "seq"), axis=0, tiled=True),
    )
    seq_count, local_rows, features = tokens.shape
    places = lax.axis_index("seq") * local_rows + jnp.arange(local_rows, dtype=jnp.int32)
    valid_mask = (
        (places[None, :] < lengths[:, None]).astype(jnp.float32).reshape(seq_count * local_rows, 1)
    )
    stream = tokens.astype(jnp.float32).reshape(seq_count * local_rows, features)
    saved_layers = []
    for which_layer in range(LAYERS):
        stream, saved = forward_layer(stream, gathered, lengths, seq_count)
        saved_layers.append(saved)
    mixed_out = (stream * valid_mask).astype(jnp.bfloat16).reshape(seq_count, local_rows, features)
    upstream = cotangent.astype(jnp.float32).reshape(seq_count * local_rows, features) * valid_mask
    gathered = (
        lax.all_gather(entry_gain, ("dp", "seq"), axis=0, tiled=True),
        lax.all_gather(entry_shift, ("dp", "seq"), axis=0, tiled=True),
        lax.all_gather(joined_weight, ("dp", "seq"), axis=0, tiled=True),
        lax.all_gather(joined_bias, ("dp", "seq"), axis=0, tiled=True),
        lax.all_gather(mixer_weight, ("dp", "seq"), axis=0, tiled=True),
        lax.all_gather(mixer_bias, ("dp", "seq"), axis=0, tiled=True),
        lax.all_gather(middle_gain, ("dp", "seq"), axis=0, tiled=True),
        lax.all_gather(middle_shift, ("dp", "seq"), axis=0, tiled=True),
        lax.all_gather(widen_weight, ("dp", "seq"), axis=0, tiled=True),
        lax.all_gather(widen_bias, ("dp", "seq"), axis=0, tiled=True),
        lax.all_gather(narrow_weight, ("dp", "seq"), axis=0, tiled=True),
        lax.all_gather(narrow_bias, ("dp", "seq"), axis=0, tiled=True),
    )
    shard_list = (
        entry_gain,
        entry_shift,
        joined_weight,
        joined_bias,
        mixer_weight,
        mixer_bias,
        middle_gain,
        middle_shift,
        widen_weight,
        widen_bias,
        narrow_weight,
        narrow_bias,
    )
    totals = tuple((jnp.zeros(one_shard.shape, jnp.float32) for one_shard in shard_list))
    for which_layer in reversed(range(LAYERS)):
        upstream, grad_terms = backward_layer(
            upstream, saved_layers[which_layer], gathered, lengths, seq_count
        )
        grad_terms = (
            lax.psum_scatter(grad_terms[0], ("dp", "seq"), scatter_dimension=0, tiled=True),
            lax.psum_scatter(grad_terms[1], ("dp", "seq"), scatter_dimension=0, tiled=True),
            lax.psum_scatter(grad_terms[2], ("dp", "seq"), scatter_dimension=0, tiled=True),
            lax.psum_scatter(grad_terms[3], ("dp", "seq"), scatter_dimension=0, tiled=True),
            lax.psum_scatter(grad_terms[4], ("dp", "seq"), scatter_dimension=0, tiled=True),
            lax.psum_scatter(grad_terms[5], ("dp", "seq"), scatter_dimension=0, tiled=True),
            lax.psum_scatter(grad_terms[6], ("dp", "seq"), scatter_dimension=0, tiled=True),
            lax.psum_scatter(grad_terms[7], ("dp", "seq"), scatter_dimension=0, tiled=True),
            lax.psum_scatter(grad_terms[8], ("dp", "seq"), scatter_dimension=0, tiled=True),
            lax.psum_scatter(grad_terms[9], ("dp", "seq"), scatter_dimension=0, tiled=True),
            lax.psum_scatter(grad_terms[10], ("dp", "seq"), scatter_dimension=0, tiled=True),
            lax.psum_scatter(grad_terms[11], ("dp", "seq"), scatter_dimension=0, tiled=True),
        )
        totals = tuple((left + right for left, right in zip(totals, grad_terms)))
    tokens_grad = upstream.astype(jnp.bfloat16).reshape(seq_count, local_rows, features)
    return (
        mixed_out,
        tokens_grad,
        totals[0],
        totals[1],
        totals[2],
        totals[3],
        totals[4],
        totals[5],
        totals[6],
        totals[7],
        totals[8],
        totals[9],
        totals[10],
        totals[11],
    )


def solution(mesh):
    return jax.shard_map(
        local,
        mesh=mesh,
        in_specs=(
            P("dp", "seq", None),
            P("dp"),
            P(("dp", "seq")),
            P(("dp", "seq")),
            P(("dp", "seq"), None),
            P(("dp", "seq")),
            P(("dp", "seq"), None),
            P(("dp", "seq")),
            P(("dp", "seq")),
            P(("dp", "seq")),
            P(("dp", "seq"), None),
            P(("dp", "seq")),
            P(("dp", "seq"), None),
            P(("dp", "seq")),
            P("dp", "seq", None),
        ),
        out_specs=(
            P("dp", "seq", None),
            P("dp", "seq", None),
            P(("dp", "seq")),
            P(("dp", "seq")),
            P(("dp", "seq"), None),
            P(("dp", "seq")),
            P(("dp", "seq"), None),
            P(("dp", "seq")),
            P(("dp", "seq")),
            P(("dp", "seq")),
            P(("dp", "seq"), None),
            P(("dp", "seq")),
            P(("dp", "seq"), None),
            P(("dp", "seq")),
        ),
        check_vma=False,
    )
```

profile of v0, /device:TPU:0, one launch (start us, length us, event | category | flops | bytes accessed | tf_op | source)
XLA Modules:
  0.0 1416.0 jit_solution(16292457735768994543)
XLA Ops:
  16.1 43.1 %all-reduce.17 = (bf16[768]{0:T(1024)(128)(2,1)S(1)}, bf16[768]{0:T(1024)(128)(2,1)S(1)}, bf16[1536]{0:T(1024)(128)(2,1)S(1)}, bf16[768]{0:T(1024)(128)(2,1)}, b...) all-reduce(bf16[768]{0:T(1024)(128)(2,1)S(1)} %dynamic-update-slice, ...), channel_id=1, replica_groups=mesh['dp'=8,'seq'=4] {'dp','seq'}, use_global_device_ids=true, to_apply=%add.1 | all-reduce | flops 9216 | bytes 36864
  100.2 30.4 %all-to-all-done = bf16[2,256,3,768]{1,0,2,3:T(2,128)(2,1)} async-done(((bf16[2,256,3,768]{1,0,2,3:T(2,128)(2,1)}), bf16[2,256,3,768]{1,0,2,3:T(2,128)(2,1)}, u32[]{:S(2)}, u32[]{:S(2)}) %all-to-all-start) | async-done | bytes 2359328 | tf_op jit(solution)/shard_map/all_to_all | solution.py:166
  141.5 114.9 %while.107 = (s32[]{:T(128)}, bf16[6,1024,64]{2,1,0:T(8,128)(2,1)}, f32[6,1024]{1,0:T(8,128)}, bf16[6,1024,64]{2,1,0:T(8,128)(2,1)}, bf16[6,1024,64]{2,1,0:T(8,1...) while((s32[]{:T(128)}, bf16[6,1024,64]{2,1,0:T(8,128)(2,1)}, ...), condition=%wide.region_7.8_spmd, body=%wide.region_2.7_spmd.sunk | while | flops 139461632 | bytes 8432610 | solution.py:178
  318.7 28.4 %all-to-all-done.2 = bf16[2,256,3,768]{1,0,2,3:T(2,128)(2,1)S(1)} async-done(((bf16[2,256,3,768]{1,0,2,3:T(2,128)(2,1)}), bf16[2,256,3,768]{1,0,2,3:T(2,128)(2,1)S(1)}, u32[]{:S(2)}, u32[]{:S(2)}) %all-to-all-start.2) | async-done | bytes 2359328 | tf_op jit(solution)/shard_map/all_to_all | solution.py:166
  354.6 79.5 %while.109 = (s32[]{:T(128)}, bf16[6,1024,64]{2,1,0:T(8,128)(2,1)}, f32[6,1024]{1,0:T(8,128)}, bf16[6,1024,64]{2,1,0:T(8,128)(2,1)}, bf16[6,1024,64]{2,1,0:T(8,1...) while((s32[]{:T(128)}, bf16[6,1024,64]{2,1,0:T(8,128)(2,1)}, ...), condition=%wide.region_17.18_spmd, body=%wide.region_12.17_spmd.sunk | while | flops 139461632 | bytes 8563562 | solution.py:178
  504.6 161.0 %while.111 = (s32[]{:T(128)}, bf16[6,1024,64]{1,2,0:T(8,128)(2,1)}, bf16[6,1024,64]{1,2,0:T(8,128)(2,1)}, bf16[6,1024,64]{1,2,0:T(8,128)(2,1)}, bf16[6,1024,64]{...) while((s32[]{:T(128)}, bf16[6,1024,64]{1,2,0:T(8,128)(2,1)}, ...), condition=%wide.region_26.27_spmd, body=%wide.region_22.26_spmd.sunk | while | flops 341804032 | bytes 24152688 | solution.py:288
  509.8 17.4 %while.116 = (s32[]{:T(128)}, f32[1024,64]{0,1:T(8,128)}, f32[1024,64]{0,1:T(8,128)}, bf16[2,512,64]{1,2,0:T(8,128)(2,1)S(1)}, s32[2]{0:T(128)S(1)}, /*index=5*/...) while((s32[]{:T(128)}, f32[1024,64]{0,1:T(8,128)}, ...), condition=%wide.region_25.25_spmd.clone, body=%wide.region_23.24_spmd.clone.sunk | while | flops 341672960 | bytes 21250904 | solution.py:123
  536.7 17.4 %while.116 = (s32[]{:T(128)}, f32[1024,64]{0,1:T(8,128)}, f32[1024,64]{0,1:T(8,128)}, bf16[2,512,64]{1,2,0:T(8,128)(2,1)S(1)}, s32[2]{0:T(128)S(1)}, /*index=5*/...) while((s32[]{:T(128)}, f32[1024,64]{0,1:T(8,128)}, ...), condition=%wide.region_25.25_spmd.clone, body=%wide.region_23.24_spmd.clone.sunk | while | flops 341672960 | bytes 21250904 | solution.py:123
  563.5 17.4 %while.116 = (s32[]{:T(128)}, f32[1024,64]{0,1:T(8,128)}, f32[1024,64]{0,1:T(8,128)}, bf16[2,512,64]{1,2,0:T(8,128)(2,1)S(1)}, s32[2]{0:T(128)S(1)}, /*index=5*/...) while((s32[]{:T(128)}, f32[1024,64]{0,1:T(8,128)}, ...), condition=%wide.region_25.25_spmd.clone, body=%wide.region_23.24_spmd.clone.sunk | while | flops 341672960 | bytes 21250904 | solution.py:123
  590.3 17.4 %while.116 = (s32[]{:T(128)}, f32[1024,64]{0,1:T(8,128)}, f32[1024,64]{0,1:T(8,128)}, bf16[2,512,64]{1,2,0:T(8,128)(2,1)S(1)}, s32[2]{0:T(128)S(1)}, /*index=5*/...) while((s32[]{:T(128)}, f32[1024,64]{0,1:T(8,128)}, ...), condition=%wide.region_25.25_spmd.clone, body=%wide.region_23.24_spmd.clone.sunk | while | flops 341672960 | bytes 21250904 | solution.py:123
  617.2 17.4 %while.116 = (s32[]{:T(128)}, f32[1024,64]{0,1:T(8,128)}, f32[1024,64]{0,1:T(8,128)}, bf16[2,512,64]{1,2,0:T(8,128)(2,1)S(1)}, s32[2]{0:T(128)S(1)}, /*index=5*/...) while((s32[]{:T(128)}, f32[1024,64]{0,1:T(8,128)}, ...), condition=%wide.region_25.25_spmd.clone, body=%wide.region_23.24_spmd.clone.sunk | while | flops 341672960 | bytes 21250904 | solution.py:123
  644.0 17.4 %while.116 = (s32[]{:T(128)}, f32[1024,64]{0,1:T(8,128)}, f32[1024,64]{0,1:T(8,128)}, bf16[2,512,64]{1,2,0:T(8,128)(2,1)S(1)}, s32[2]{0:T(128)S(1)}, /*index=5*/...) while((s32[]{:T(128)}, f32[1024,64]{0,1:T(8,128)}, ...), condition=%wide.region_25.25_spmd.clone, body=%wide.region_23.24_spmd.clone.sunk | while | flops 341672960 | bytes 21250904 | solution.py:123
  677.3 36.9 %all-to-all-done.5 = bf16[2,1024,3,192]{3,0,2,1:T(2,128)(2,1)S(1)} async-done(((bf16[2,1024,3,192]{3,0,2,1:T(2,128)(2,1)}), bf16[2,1024,3,192]{3,0,2,1:T(2,128)(2,1)S(1)}, u32[]{:S(2)}, u32[]{:S(2)}) %all-to-all-start.5) | async-done | bytes 2359328 | tf_op jit(solution)/shard_map/all_to_all | solution.py:300
  774.6 161.1 %while.113 = (s32[]{:T(128)}, bf16[6,1024,64]{1,2,0:T(8,128)(2,1)}, bf16[6,1024,64]{1,2,0:T(8,128)(2,1)}, bf16[6,1024,64]{1,2,0:T(8,128)(2,1)}, bf16[6,1024,64]{...) while((s32[]{:T(128)}, bf16[6,1024,64]{1,2,0:T(8,128)(2,1)}, ...), condition=%wide.region_35.36_spmd, body=%wide.region_31.35_spmd.sunk | while | flops 341804032 | bytes 24152688 | solution.py:288
  779.8 17.4 %while.117 = (s32[]{:T(128)}, f32[1024,64]{0,1:T(8,128)}, f32[1024,64]{0,1:T(8,128)}, bf16[2,512,64]{1,2,0:T(8,128)(2,1)S(1)}, s32[2]{0:T(128)S(1)}, /*index=5*/...) while((s32[]{:T(128)}, f32[1024,64]{0,1:T(8,128)}, ...), condition=%wide.region_34.34_spmd.clone, body=%wide.region_32.33_spmd.clone.sunk | while | flops 341672960 | bytes 21250904 | solution.py:123
  806.6 17.5 %while.117 = (s32[]{:T(128)}, f32[1024,64]{0,1:T(8,128)}, f32[1024,64]{0,1:T(8,128)}, bf16[2,512,64]{1,2,0:T(8,128)(2,1)S(1)}, s32[2]{0:T(128)S(1)}, /*index=5*/...) while((s32[]{:T(128)}, f32[1024,64]{0,1:T(8,128)}, ...), condition=%wide.region_34.34_spmd.clone, body=%wide.region_32.33_spmd.clone.sunk | while | flops 341672960 | bytes 21250904 | solution.py:123
  833.5 17.4 %while.117 = (s32[]{:T(128)}, f32[1024,64]{0,1:T(8,128)}, f32[1024,64]{0,1:T(8,128)}, bf16[2,512,64]{1,2,0:T(8,128)(2,1)S(1)}, s32[2]{0:T(128)S(1)}, /*index=5*/...) while((s32[]{:T(128)}, f32[1024,64]{0,1:T(8,128)}, ...), condition=%wide.region_34.34_spmd.clone, body=%wide.region_32.33_spmd.clone.sunk | while | flops 341672960 | bytes 21250904 | solution.py:123
  860.4 17.4 %while.117 = (s32[]{:T(128)}, f32[1024,64]{0,1:T(8,128)}, f32[1024,64]{0,1:T(8,128)}, bf16[2,512,64]{1,2,0:T(8,128)(2,1)S(1)}, s32[2]{0:T(128)S(1)}, /*index=5*/...) while((s32[]{:T(128)}, f32[1024,64]{0,1:T(8,128)}, ...), condition=%wide.region_34.34_spmd.clone, body=%wide.region_32.33_spmd.clone.sunk | while | flops 341672960 | bytes 21250904 | solution.py:123
  887.2 17.4 %while.117 = (s32[]{:T(128)}, f32[1024,64]{0,1:T(8,128)}, f32[1024,64]{0,1:T(8,128)}, bf16[2,512,64]{1,2,0:T(8,128)(2,1)S(1)}, s32[2]{0:T(128)S(1)}, /*index=5*/...) while((s32[]{:T(128)}, f32[1024,64]{0,1:T(8,128)}, ...), condition=%wide.region_34.34_spmd.clone, body=%wide.region_32.33_spmd.clone.sunk | while | flops 341672960 | bytes 21250904 | solution.py:123
  914.1 17.4 %while.117 = (s32[]{:T(128)}, f32[1024,64]{0,1:T(8,128)}, f32[1024,64]{0,1:T(8,128)}, bf16[2,512,64]{1,2,0:T(8,128)(2,1)S(1)}, s32[2]{0:T(128)S(1)}, /*index=5*/...) while((s32[]{:T(128)}, f32[1024,64]{0,1:T(8,128)}, ...), condition=%wide.region_34.34_spmd.clone, body=%wide.region_32.33_spmd.clone.sunk | while | flops 341672960 | bytes 21250904 | solution.py:123
  956.4 28.8 %all-to-all-done.7 = bf16[2,1024,3,192]{3,0,2,1:T(2,128)(2,1)} async-done(((bf16[2,1024,3,192]{3,0,2,1:T(2,128)(2,1)}), bf16[2,1024,3,192]{3,0,2,1:T(2,128)(2,1)}, u32[]{:S(2)}, u32[]{:S(2)}) %all-to-all-start.7) | async-done | bytes 2359328 | tf_op jit(solution)/shard_map/all_to_all | solution.py:300
  1067.8 39.8 %all-reduce.16 = (f32[768]{0:T(1024)S(1)}, f32[768]{0:T(1024)S(1)}, f32[1536]{0:T(1024)S(1)}, f32[768]{0:T(1024)S(1)}, f32[768]{0:T(1024)S(1)}, /*index=5*/f32[7...) all-reduce(f32[768]{0:T(1024)S(1)} %add.434, ...), channel_id=14, replica_groups=mesh['dp'=8,'seq'=4] {'dp','seq'}, use_global_device_ids=true, to_apply=%region_39.40.clone | all-reduce | flops 9216 | bytes 73728
  1125.3 141.8 %reduce-scatter.11.cloned.1.call-done = f32[96,768]{1,0:T(8,128)} async-done(((f32[3072,768]{1,0:T(8,128)}), f32[96,768]{1,0:T(8,128)}) %reduce-scatter.11.cloned.1.call-update) | async-done | bytes 294928 | tf_op jit(solution)/shard_map/reduce_scatter | solution.py:420
  1267.1 141.6 %reduce-scatter.9.cloned.1.call-done = f32[24,3072]{1,0:T(8,128)} async-done(((f32[768,3072]{1,0:T(8,128)}), f32[24,3072]{1,0:T(8,128)}) %reduce-scatter.9.cloned.1.call-update) | async-done | bytes 294928 | tf_op jit(solution)/shard_map/reduce_scatter | solution.py:418
  (1536 shorter events, 1023.7 us)
Async XLA Ops:
  7.2 56.1 %copy-start.12 = (bf16[2,256,768]{2,1,0:T(8,128)(2,1)S(1)}, bf16[2,256,768]{2,1,0:T(8,128)(2,1)}, u32[]{:S(2)}) copy-start(bf16[2,256,768]{2,1,0:T(8,128)(2,1)} %param.31) | copy-start | bytes 2359300
  7.2 66.6 %all-gather.5.cloned.1.call-start = ((), (), s32[]{:S(2)}) async-start(), calls=%async_computation.12 | async-start | bytes 3649536 | tf_op jit(solution)/shard_map/all_gather | solution.py:353
  7.9 273.3 %all-gather.7.cloned.1.call-start = ((), (), s32[]{:S(2)}) async-start(), calls=%async_computation.13 | async-start | bytes 1216512 | tf_op jit(solution)/shard_map/all_gather | solution.py:355
  8.7 275.4 %all-gather.9.cloned.1.call-start = ((), (), s32[]{:S(2)}) async-start(), calls=%async_computation.14 | async-start | bytes 4866048 | tf_op jit(solution)/shard_map/all_gather | solution.py:359
  59.3 240.7 %copy-start.47 = (f32[768]{0:T(1024)}, f32[768]{0:T(1024)S(1)}, u32[]{:S(2)}) copy-start(f32[768]{0:T(1024)S(1)} %convert_element_type.211) | copy-start | bytes 9220
  94.3 36.3 %all-to-all-start = ((bf16[2,256,3,768]{1,0,2,3:T(2,128)(2,1)}), bf16[2,256,3,768]{1,0,2,3:T(2,128)(2,1)}, u32[]{:S(2)}, u32[]{:S(2)}) async-start(bf16[2,256,3,768]{1,0,2,3:T(2,128)(2,1)} %copy.82), calls=%async_computation | async-start | bytes 4718592 | tf_op jit(solution)/shard_map/all_to_all | solution.py:166
  98.9 192.9 %all-gather.11.cloned.1.call-start = ((), (), s32[]{:S(2)}) async-start(), calls=%async_computation.15 | async-start | bytes 4866048 | tf_op jit(solution)/shard_map/all_gather | solution.py:361
  260.2 18.4 %all-to-all-start.1 = ((bf16[2,1024,192]{2,0,1:T(2,128)(2,1)}), bf16[2,1024,192]{2,0,1:T(2,128)(2,1)S(1)}, u32[]{:S(2)}, u32[]{:S(2)}) async-start(bf16[2,1024,192]{2,0,1:T(2,128)(2,1)} %copy.89), calls=%async_computation.1 | async-start | bytes 2097152 | tf_op jit(solution)/shard_map/all_to_all | solution.py:179
  264.2 215.0 %copy-start.44 = (f32[768]{0:T(1024)}, f32[768]{0:T(1024)S(1)}, u32[]{:S(2)}) copy-start(f32[768]{0:T(1024)S(1)} %convert_element_type.218) | copy-start | bytes 9220
  264.3 199.1 %copy-start.50 = (f32[768]{0:T(1024)}, f32[768]{0:T(1024)S(1)}, u32[]{:S(2)}) copy-start(f32[768]{0:T(1024)S(1)} %convert_element_type.219) | copy-start | bytes 9220
  264.3 204.1 %copy-start.88 = (f32[3072]{0:T(1024)}, f32[3072]{0:T(1024)S(1)}, u32[]{:S(2)}) copy-start(f32[3072]{0:T(1024)S(1)} %convert_element_type.221) | copy-start | bytes 36868
  315.1 32.1 %all-to-all-start.2 = ((bf16[2,256,3,768]{1,0,2,3:T(2,128)(2,1)}), bf16[2,256,3,768]{1,0,2,3:T(2,128)(2,1)S(1)}, u32[]{:S(2)}, u32[]{:S(2)}) async-start(bf16[2,256,3,768]{1,0,2,3:T(2,128)(2,1)} %copy.92), calls=%async_computation.2 | async-start | bytes 4718592 | tf_op jit(solution)/shard_map/all_to_all | solution.py:166
  437.9 18.1 %all-to-all-start.3 = ((bf16[2,1024,192]{2,0,1:T(2,128)(2,1)}), bf16[2,1024,192]{2,0,1:T(2,128)(2,1)S(1)}, u32[]{:S(2)}, u32[]{:S(2)}) async-start(bf16[2,1024,192]{2,0,1:T(2,128)(2,1)} %copy.99), calls=%async_computation.3 | async-start | bytes 2097152 | tf_op jit(solution)/shard_map/all_to_all | solution.py:179
  442.2 37.7 %copy-start.62 = (f32[1,2,2,128]{3,1,2,0:T(2,128)}, f32[1,2,2,128]{3,1,2,0:T(2,128)S(1)}, u32[]{:S(2)}) copy-start(f32[1,2,2,128]{3,1,2,0:T(2,128)S(1)} %copy.143) | copy-start | bytes 6148
  484.4 15.1 %all-to-all-start.4 = ((bf16[2,256,768]{1,0,2:T(2,128)(2,1)}), bf16[2,256,768]{1,0,2:T(2,128)(2,1)S(1)}, u32[]{:S(2)}, u32[]{:S(2)}) async-start(bf16[2,256,768]{1,0,2:T(2,128)(2,1)} %copy.101), calls=%async_computation.4 | async-start | bytes 1572864 | tf_op jit(solution)/shard_map/all_to_all | solution.py:279
  673.3 40.8 %all-to-all-start.5 = ((bf16[2,1024,3,192]{3,0,2,1:T(2,128)(2,1)}), bf16[2,1024,3,192]{3,0,2,1:T(2,128)(2,1)S(1)}, u32[]{:S(2)}, u32[]{:S(2)}) async-start(bf16[2,1024,3,192]{3,0,2,1:T(2,128)(2,1)} %copy.111), calls=%async_computation.5 | async-start | bytes 6291456 | tf_op jit(solution)/shard_map/all_to_all | solution.py:300
  754.3 15.1 %all-to-all-start.6 = ((bf16[2,256,768]{1,0,2:T(2,128)(2,1)}), bf16[2,256,768]{1,0,2:T(2,128)(2,1)S(1)}, u32[]{:S(2)}, u32[]{:S(2)}) async-start(bf16[2,256,768]{1,0,2:T(2,128)(2,1)} %copy.113), calls=%async_computation.6 | async-start | bytes 1572864 | tf_op jit(solution)/shard_map/all_to_all | solution.py:279
  757.9 357.8 %reduce-scatter.7.cloned.1.call-start = ((), (), s32[]{:S(2)}) async-start(), calls=%async_computation.17 | async-start | bytes 2433024 | tf_op jit(solution)/shard_map/reduce_scatter | solution.py:414
  943.4 41.8 %all-to-all-start.7 = ((bf16[2,1024,3,192]{3,0,2,1:T(2,128)(2,1)}), bf16[2,1024,3,192]{3,0,2,1:T(2,128)(2,1)}, u32[]{:S(2)}, u32[]{:S(2)}) async-start(bf16[2,1024,3,192]{3,0,2,1:T(2,128)(2,1)} %copy.123), calls=%async_computation.7 | async-start | bytes 6291456 | tf_op jit(solution)/shard_map/all_to_all | solution.py:300
  948.2 177.1 %reduce-scatter.5.cloned.1.call-start = ((), (), s32[]{:S(2)}) async-start(), calls=%async_computation.16 | async-start | bytes 7299072 | tf_op jit(solution)/shard_map/reduce_scatter | solution.py:412
  1006.6 260.5 %reduce-scatter.11.cloned.1.call-start = ((), (), s32[]{:S(2)}) async-start(), calls=%async_computation.19 | async-start | bytes 9732096 | tf_op jit(solution)/shard_map/reduce_scatter | solution.py:420
  1024.3 384.5 %reduce-scatter.9.cloned.1.call-start = ((), (), s32[]{:S(2)}) async-start(), calls=%async_computation.18 | async-start | bytes 9732096 | tf_op jit(solution)/shard_map/reduce_scatter | solution.py:418
  1065.8 46.4 %copy-start.21 = (f32[512,768]{1,0:T(8,128)S(1)}, f32[512,768]{1,0:T(8,128)}, u32[]{:S(2)}) copy-start(f32[512,768]{1,0:T(8,128)} %copy-done.19) | copy-start | bytes 4718596
  1065.8 46.4 %copy-start.69 = (f32[512]{0:T(512)S(1)}, f32[512]{0:T(512)}, u32[]{:S(2)}) copy-start(f32[512]{0:T(512)} %copy-done.68) | copy-start | bytes 6148
  (280 other events, 1040.0 us)
Sparse Core Ops, SparseCore 0:
  10.9 62.8 all-gather.4
  76.7 54.8 all-gather.6
  134.4 62.6 all-gather.8
  199.9 61.9 all-gather.10
  764.2 99.9 reduce-scatter.6
  1006.7 118.5 reduce-scatter.4
  1131.8 135.2 reduce-scatter.10
  1273.6 135.1 reduce-scatter.8
where the time goes:
time: 1430 us; the launch traced here: 1420 us
  waiting for transfers between devices  476 us (33%)
  local copies, waits for them, and re-layouts  331 us (23%)
  matrix products  321 us (22%)
  other arithmetic  152 us (11%)
  blocking collectives  82.9 us (6%)
  starting transfers between devices  32.5 us (2%)
  between operations  16.4 us (1%)
    reduce_scatter x1, waiting for transfers between devices, local(): lax.psum_scatter(grad_terms[10], ('dp', 'seq'), scatter_dimension=0, tile...  142 us
    reduce_scatter x1, waiting for transfers between devices, local(): lax.psum_scatter(grad_terms[8], ('dp', 'seq'), scatter_dimension=0, tiled...  142 us
    unnamed x2, blocking collectives  82.9 us
    dynamic_slice x72, local copies, waits for them, and re-layouts, forward_layer(): lax.map(attend_forward, (queries, key_rows, values, item_lengths))  66.3 us
    all_to_all x2, waiting for transfers between devices, backward_layer(): lax.all_to_all(stacked, 'seq', split_axis=1, concat_axis=3, tiled=True)  65.6 us
    all_to_all x2, waiting for transfers between devices, forward_layer(): lax.all_to_all(joined_rows.reshape(seq_count, local_rows, 3, features), '...  58.9 us
    dot_general x48, matrix products, one_block(): jnp.einsum('qd,kd->qk', query_block, key_rows, preferred_element_type=jnp...  49.6 us
    dot_general x24, matrix products, one_block(): jnp.einsum('qk,qd->kd', score_grad, query_block, preferred_element_type=j...  48.4 us
  transfers between devices with their start and end apart: 16, of which 12 were waited for; matrix products, arithmetic and copies ran while one was open for 31% of the time, Pallas kernels for 0%

commit v1 on v0

--- a/solution.py
+++ b/solution.py
@@ -1,15 +1,26 @@
+import functools
+
 import jax
 import jax.numpy as jnp
 from jax import lax
+from jax.experimental import pallas as pl
+from jax.experimental.pallas import tpu as pltpu
 from jax.sharding import PartitionSpec as P
 
 HD = 64
 LAYERS = 2
-
-
 EPSILON = 1e-05
 NEGATIVE = -1e30
-BLOCK_LIMIT = 512
+f32 = jnp.float32
+bf16 = jnp.bfloat16
+NN = ((1,), (0,))
+NT = ((1,), (1,))
+TN = ((0,), (0,))
+TT = ((0,), (1,))
+
+
+def dot(left, right, dims):
+    return lax.dot_general(left, right, (dims, ((), ())), preferred_element_type=f32)
 
 
 def layer_norm(inputs, gain_row, shift_row):
@@ -23,118 +34,144 @@
     return jax.nn.gelu(values, approximate=True)
 
 
-def to_items(packed, heads_here):
-    seq_count, total_rows, features = packed.shape
-    head_size = features // heads_here
-    return (
-        packed.reshape(seq_count, total_rows, heads_here, head_size)
-        .transpose(0, 2, 1, 3)
-        .reshape(seq_count * heads_here, total_rows, head_size)
-    )
-
-
-def from_items(items, seq_count):
-    item_count, total_rows, head_size = items.shape
-    heads_here = item_count // seq_count
-    return (
-        items.reshape(seq_count, heads_here, total_rows, head_size)
-        .transpose(0, 2, 1, 3)
-        .reshape(seq_count, total_rows, heads_here * head_size)
-    )
-
-
-def block_mask(first_row, block_rows, length, total_rows):
-    query_places = first_row + jnp.arange(block_rows, dtype=jnp.int32)[:, None]
-    key_places = jnp.arange(total_rows, dtype=jnp.int32)[None, :]
-    return (key_places <= query_places) & (key_places < length)
-
-
-def attend_forward(packet):
-    queries, key_rows, values, length = packet
-    total_rows, head_size = queries.shape
-    block_rows = min(BLOCK_LIMIT, total_rows)
-    block_count = total_rows // block_rows
-    scaling = head_size ** (-0.5)
-
-    def one_block(portion):
-        query_block, first_row = portion
-        scores = (
-            jnp.einsum("qd,kd->qk", query_block, key_rows, preferred_element_type=jnp.float32)
-            * scaling
-        )
-        masked = jnp.where(block_mask(first_row, block_rows, length, total_rows), scores, NEGATIVE)
-        row_top = jnp.max(masked, axis=1, keepdims=True)
-        lifted = jnp.exp(masked - row_top)
-        summed = jnp.sum(lifted, axis=1, keepdims=True)
-        shares = (lifted / summed).astype(jnp.bfloat16)
-        result = jnp.einsum("qk,kd->qd", shares, values, preferred_element_type=jnp.float32)
-        return (result, (row_top + jnp.log(summed))[:, 0])
-
-    starts = jnp.arange(block_count, dtype=jnp.int32) * block_rows
-    results, logsum = lax.map(
-        one_block, (queries.reshape(block_count, block_rows, head_size), starts)
-    )
-    return (results.reshape(total_rows, head_size), logsum.reshape(total_rows))
-
-
-def attend_backward(packet):
-    queries, key_rows, values, upstream, logsum, length = packet
-    total_rows, head_size = queries.shape
-    block_rows = min(BLOCK_LIMIT, total_rows)
-    block_count = total_rows // block_rows
-    scaling = head_size ** (-0.5)
-
-    def one_block(running, portion):
-        key_sum, value_sum = running
-        query_block, upstream_block, logsum_block, first_row = portion
-        scores = (
-            jnp.einsum("qd,kd->qk", query_block, key_rows, preferred_element_type=jnp.float32)
-            * scaling
-        )
-        shares = jnp.where(
-            block_mask(first_row, block_rows, length, total_rows),
-            jnp.exp(scores - logsum_block[:, None]),
-            0.0,
-        )
-        value_sum = value_sum + jnp.einsum(
-            "qk,qd->kd",
-            shares.astype(jnp.bfloat16),
-            upstream_block,
-            preferred_element_type=jnp.float32,
-        )
-        share_grad = jnp.einsum(
-            "qd,kd->qk", upstream_block, values, preferred_element_type=jnp.float32
-        )
-        centre = jnp.sum(share_grad * shares, axis=1, keepdims=True)
-        score_grad = (shares * (share_grad - centre)).astype(jnp.bfloat16)
-        query_grad = (
-            jnp.einsum("qk,kd->qd", score_grad, key_rows, preferred_element_type=jnp.float32)
-            * scaling
-        )
-        key_sum = (
-            key_sum
-            + jnp.einsum("qk,qd->kd", score_grad, query_block, preferred_element_type=jnp.float32)
-            * scaling
-        )
-        return ((key_sum, value_sum), query_grad)
-
-    zero_rows = jnp.zeros((total_rows, head_size), jnp.float32)
-    starts = jnp.arange(block_count, dtype=jnp.int32) * block_rows
-    (key_sum, value_sum), query_grads = lax.scan(
-        one_block,
-        (zero_rows, zero_rows),
-        (
-            queries.reshape(block_count, block_rows, head_size),
-            upstream.reshape(block_count, block_rows, head_size),
-            logsum.reshape(block_count, block_rows),
-            starts,
-        ),
-    )
-    return (
-        query_grads.reshape(total_rows, head_size).astype(jnp.bfloat16),
-        key_sum.astype(jnp.bfloat16),
-        value_sum.astype(jnp.bfloat16),
-    )
+def causal_mask(first, rows, length):
+    keys = lax.broadcasted_iota(jnp.int32, (rows, rows), 0)
+    queries = lax.broadcasted_iota(jnp.int32, (rows, rows), 1)
+    return (keys <= queries) & (keys + first < length)
+
+
+def attend_forward_body(n, rows, len_ref, q_ref, k_ref, v_ref, o_ref, l_ref):
+    length = len_ref[pl.program_id(0)]
+    hd = q_ref.shape[3]
+    keys = [k_ref[j, 0, 0].T for j in range(n)]
+    for i in range(n):
+
+        @pl.when(i * rows < length)
+        def _():
+            query = q_ref[i, 0, 0] * jnp.asarray(hd**-0.5, bf16)
+            scores = []
+            for j in range(i + 1):
+                block = dot(keys[j], query, NN)
+                if j == i:
+                    block = jnp.where(causal_mask(j * rows, rows, length), block, NEGATIVE)
+                scores.append(block)
+            top = scores[0].max(axis=0, keepdims=True)
+            for j in range(1, i + 1):
+                top = jnp.maximum(top, scores[j].max(axis=0, keepdims=True))
+            total = jnp.zeros((1, rows), f32)
+            out = jnp.zeros((hd, rows), f32)
+            for j in range(i + 1):
+                lifted = jnp.exp(scores[j] - top)
+                total = total + lifted.sum(axis=0, keepdims=True)
+                out = out + dot(v_ref[j, 0, 0], lifted.astype(bf16), NN)
+            o_ref[i, 0] = (out / total).astype(bf16)
+            l_ref[0, 0, i : i + 1, :] = top + jnp.log(total)
+
+        @pl.when(i * rows >= length)
+        def _():
+            o_ref[i, 0] = jnp.zeros((hd, rows), bf16)
+            l_ref[0, 0, i : i + 1, :] = jnp.zeros((1, rows), f32)
+
+
+def attend_backward_body(
+    n, rows, len_ref, q_ref, k_ref, v_ref, g_ref, o_ref, l_ref, d_ref, dk_acc, dv_acc
+):
+    length = len_ref[pl.program_id(0)]
+    hd = q_ref.shape[3]
+    keys = [k_ref[j, 0, 0].T for j in range(n)]
+    vals = [v_ref[j, 0, 0].T for j in range(n)]
+    dk_acc[...] = jnp.zeros_like(dk_acc)
+    dv_acc[...] = jnp.zeros_like(dv_acc)
+    for i in range(n):
+
+        @pl.when(i * rows < length)
+        def _():
+            query = q_ref[i, 0, 0]
+            scaled = query * jnp.asarray(hd**-0.5, bf16)
+            grad = g_ref[i, 0]
+            scaled_rows = scaled.T
+            grad_rows = grad.T
+            logsum = l_ref[0, 0, i : i + 1, :]
+            centre = (grad.astype(f32) * o_ref[i, 0].astype(f32)).sum(axis=0, keepdims=True)
+            dq = jnp.zeros((hd, rows), f32)
+            for j in range(i + 1):
+                share = jnp.exp(dot(keys[j], scaled, NN) - logsum)
+                if j == i:
+                    share = jnp.where(causal_mask(j * rows, rows, length), share, 0.0)
+                share_grad = dot(vals[j], grad, NN)
+                score_grad = (share * (share_grad - centre)).astype(bf16)
+                dv_acc[j] += dot(share.astype(bf16), grad_rows, NN)
+                dk_acc[j] += dot(score_grad, scaled_rows, NN)
+                dq = dq + dot(k_ref[j, 0, 0], score_grad, NN)
+            d_ref[i, 0, 0] = (dq * (hd**-0.5)).astype(bf16)
+
+        @pl.when(i * rows >= length)
+        def _():
+            d_ref[i, 0, 0] = jnp.zeros((hd, rows), bf16)
+
+    for j in range(n):
+        d_ref[j, 1, 0] = dk_acc[j].astype(bf16).T
+        d_ref[j, 2, 0] = dv_acc[j].astype(bf16).T
+
+
+def attention_specs(packed, seqs):
+    n, _, heads, hd, cols = packed.shape
+    rows = cols // seqs
+
+    def part(which):
+        return pl.BlockSpec((n, 1, 1, hd, rows), lambda b, h, L: (0, which, h, 0, b))
+
+    item = pl.BlockSpec((n, 1, hd, rows), lambda b, h, L: (0, h, 0, b))
+    line = pl.BlockSpec((1, 1, n, rows), lambda b, h, L: (b, h, 0, 0))
+    return n, heads, hd, cols, rows, part, item, line
+
+
+def attend_forward(packed, lengths):
+    seqs = lengths.shape[0]
+    n, heads, hd, cols, rows, part, item, line = attention_specs(packed, seqs)
+    blocks = seqs * heads * n * (n + 1) // 2
+    return pl.pallas_call(
+        functools.partial(attend_forward_body, n, rows),
+        grid_spec=pltpu.PrefetchScalarGridSpec(
+            num_scalar_prefetch=1,
+            grid=(seqs, heads),
+            in_specs=[part(0), part(1), part(2)],
+            out_specs=[item, line],
+        ),
+        out_shape=[
+            jax.ShapeDtypeStruct((n, heads, hd, cols), bf16),
+            jax.ShapeDtypeStruct((seqs, heads, n, rows), f32),
+        ],
+        cost_estimate=pl.CostEstimate(
+            flops=4 * blocks * rows * rows * hd,
+            bytes_accessed=4 * n * heads * hd * cols * 2,
+            transcendentals=blocks * rows * rows,
+        ),
+        name="attend_forward",
+    )(lengths, packed, packed, packed)
+
+
+def attend_backward(packed, grad, out, logsum, lengths):
+    seqs = lengths.shape[0]
+    n, heads, hd, cols, rows, part, item, line = attention_specs(packed, seqs)
+    blocks = seqs * heads * n * (n + 1) // 2
+    return pl.pallas_call(
+        functools.partial(attend_backward_body, n, rows),
+        grid_spec=pltpu.PrefetchScalarGridSpec(
+            num_scalar_prefetch=1,
+            grid=(seqs, heads),
+            in_specs=[part(0), part(1), part(2), item, item, line],
+            out_specs=pl.BlockSpec((n, 3, 1, hd, rows), lambda b, h, L: (0, 0, h, 0, b)),
+            scratch_shapes=[pltpu.VMEM((n, rows, hd), f32), pltpu.VMEM((n, rows, hd), f32)],
+        ),
+        out_shape=jax.ShapeDtypeStruct((n, 3, heads, hd, cols), bf16),
+        cost_estimate=pl.CostEstimate(
+            flops=10 * blocks * rows * rows * hd,
+            bytes_accessed=8 * n * heads * hd * cols * 2,
+            transcendentals=blocks * rows * rows,
+        ),
+        name="attend_backward",
+    )(lengths, packed, packed, packed, grad, out, logsum)
 
 
 def forward_layer(stream, gathered, lengths, seq_count):
@@ -157,36 +194,19 @@
     normed = layer_norm(
         stream, entry_gain.astype(jnp.float32), entry_shift.astype(jnp.float32)
     ).astype(jnp.bfloat16)
+    groups = lax.axis_size("seq")
     bias_row = jnp.concatenate(
         [joined_bias[:features], jnp.zeros((features,), jnp.bfloat16), joined_bias[features:]]
     ).astype(jnp.float32)
-    joined_rows = (
-        jnp.dot(normed, joined_weight, preferred_element_type=jnp.float32) + bias_row
-    ).astype(jnp.bfloat16)
-    headed = lax.all_to_all(
-        joined_rows.reshape(seq_count, local_rows, 3, features),
-        "seq",
-        split_axis=3,
-        concat_axis=1,
-        tiled=True,
-    )
-    heads_here = headed.shape[3] // HD
-    queries = to_items(headed[:, :, 0], heads_here)
-    key_rows = to_items(headed[:, :, 1], heads_here)
-    values = to_items(headed[:, :, 2], heads_here)
-    item_lengths = jnp.repeat(lengths, heads_here)
-    mixed_rows, logsum = lax.map(attend_forward, (queries, key_rows, values, item_lengths))
-    returned = lax.all_to_all(
-        from_items(mixed_rows.astype(jnp.bfloat16), seq_count),
-        "seq",
-        split_axis=1,
-        concat_axis=2,
-        tiled=True,
-    )
-    attended = returned.reshape(seq_count * local_rows, features)
+    bias_row = bias_row.reshape(3, groups, features // groups).transpose(1, 0, 2).reshape(-1, 1)
+    joined_rows = (dot(joined_weight, normed, TT) + bias_row).astype(jnp.bfloat16)
+    heads_here = features // groups // HD
+    packed = swap_groups(joined_rows.reshape(groups, 3, heads_here, HD, stream.shape[0]))
+    mixed, logsum = attend_forward(packed, lengths)
+    attended = swap_groups(mixed).reshape(features, stream.shape[0])
     middle = (
         stream
-        + jnp.dot(attended, mixer_weight, preferred_element_type=jnp.float32)
+        + dot(attended, mixer_weight, TN)
         + mixer_bias.astype(jnp.float32)
     )
     normed_two = layer_norm(
@@ -204,9 +224,8 @@
     saved = (
         stream,
         normed,
-        queries,
-        key_rows,
-        values,
+        packed,
+        mixed,
         logsum,
         attended,
         middle,
@@ -235,9 +254,8 @@
     (
         stream,
         normed,
-        queries,
-        key_rows,
-        values,
+        packed,
+        mixed,
         logsum,
         attended,
         middle,
@@ -269,45 +287,20 @@
     middle_grad, middle_gain_term, middle_shift_term = middle_pull(normed_two_grad)
     middle_grad = middle_grad + upstream
     mixer_grad = middle_grad.astype(jnp.bfloat16)
-    mixer_weight_term = jnp.einsum(
-        "te,td->ed", attended, mixer_grad, preferred_element_type=jnp.float32
-    )
+    mixer_weight_term = dot(attended, mixer_grad, NN)
     mixer_bias_term = jnp.sum(mixer_grad.astype(jnp.float32), axis=0)
-    attended_grad = jnp.einsum(
-        "td,ed->te", mixer_grad, mixer_weight, preferred_element_type=jnp.float32
-    ).astype(jnp.bfloat16)
-    heads_grad = lax.all_to_all(
-        attended_grad.reshape(seq_count, local_rows, features),
-        "seq",
-        split_axis=2,
-        concat_axis=1,
-        tiled=True,
-    )
-    heads_here = heads_grad.shape[2] // HD
-    item_lengths = jnp.repeat(lengths, heads_here)
-    query_grad, key_grad, value_grad = lax.map(
-        attend_backward,
-        (queries, key_rows, values, to_items(heads_grad, heads_here), logsum, item_lengths),
-    )
-    stacked = jnp.stack(
-        [
-            from_items(query_grad, seq_count),
-            from_items(key_grad, seq_count),
-            from_items(value_grad, seq_count),
-        ],
-        axis=2,
-    )
-    joined_grad = lax.all_to_all(stacked, "seq", split_axis=1, concat_axis=3, tiled=True).reshape(
-        seq_count * local_rows, 3 * features
-    )
-    joined_weight_term = jnp.einsum(
-        "td,te->de", normed, joined_grad, preferred_element_type=jnp.float32
-    )
-    joined_sums = jnp.sum(joined_grad.astype(jnp.float32), axis=0)
-    joined_bias_term = jnp.concatenate([joined_sums[:features], joined_sums[2 * features :]])
-    normed_grad = jnp.einsum(
-        "te,de->td", joined_grad, joined_weight, preferred_element_type=jnp.float32
-    )
+    attended_grad = dot(mixer_weight, mixer_grad, NT).astype(jnp.bfloat16)
+    groups = lax.axis_size("seq")
+    heads_grad = swap_groups(attended_grad.reshape(mixed.shape))
+    packed_grad = attend_backward(packed, heads_grad, mixed, logsum, lengths)
+    joined_grad = swap_groups(packed_grad).reshape(3 * features, stream.shape[0])
+    joined_weight_term = dot(normed, joined_grad, TT)
+    joined_sums = jnp.sum(joined_grad.astype(jnp.float32), axis=1)
+    joined_sums = (
+        joined_sums.reshape(groups, 3, features // groups).transpose(1, 0, 2).reshape(3, features)
+    )
+    joined_bias_term = jnp.concatenate([joined_sums[0], joined_sums[2]])
+    normed_grad = dot(joined_grad, joined_weight, TT)
     entry_pull = jax.vjp(
         layer_norm, stream, entry_gain.astype(jnp.float32), entry_shift.astype(jnp.float32)
     )[1]
@@ -330,6 +323,10 @@
     return (stream_grad, grad_terms)
 
 
+def swap_groups(blocks):
+    return lax.all_to_all(blocks, "seq", split_axis=0, concat_axis=0, tiled=True)
+
+
 def local(
     tokens,
     lengths,
@@ -347,6 +344,11 @@
     narrow_bias,
     cotangent,
 ):
+    groups = lax.axis_size("seq")
+    rows_here = joined_weight.shape[0]
+    joined_weight = (
+        joined_weight.reshape(rows_here, 3, groups, -1).transpose(0, 2, 1, 3).reshape(rows_here, -1)
+    )
     gathered = (
         lax.all_gather(entry_gain, ("dp", "seq"), axis=0, tiled=True),
         lax.all_gather(entry_shift, ("dp", "seq"), axis=0, tiled=True),
@@ -421,6 +423,10 @@
             lax.psum_scatter(grad_terms[11], ("dp", "seq"), scatter_dimension=0, tiled=True),
         )
         totals = tuple((left + right for left, right in zip(totals, grad_terms)))
+    totals = list(totals)
+    totals[2] = (
+        totals[2].reshape(rows_here, groups, 3, -1).transpose(0, 2, 1, 3).reshape(rows_here, -1)
+    )
     tokens_grad = upstream.astype(jnp.bfloat16).reshape(seq_count, local_rows, features)
     return (
         mixed_out,

time: 1430 us -> 1050 us (0.73)
  local copies, waits for them, and re-layouts: 331 us -> 31.5 us
  matrix products: 321 us -> 122 us
  other arithmetic: 152 us -> 13.8 us
  waiting for transfers between devices: 476 us -> 598 us
  blocking collectives: 82.9 us -> 196 us
  Pallas kernels: 0 us -> 54.1 us
  starting transfers between devices: 32.5 us -> 16.2 us
    dot_general x180 -> x12, matrix products: 242 us -> 44.2 us  [dot(): lax.dot_general(left, right, (dims, ((), ())), preferred_element_type=f32)]
    dynamic_slice x156 -> x0, local copies, waits for them, and re-layouts: 107 us -> none  [the longest x72 66.3 us: forward_layer(): lax.map(attend_forward, (queries, key_rows, values, item_lengths))]
    reduce_scatter x1, waiting for transfers between devices: 0.01 us -> 102 us  [local(): lax.psum_scatter(grad_terms[4], ('dp', 'seq'), scatter_dimension=0, tiled...]
    all_to_all x8 -> x4, waiting for transfers between devices: 170 us -> 70.1 us  [swap_groups(): lax.all_to_all(blocks, 'seq', split_axis=0, concat_axis=0, tiled=True)]
    all_to_all x0 -> x4, blocking collectives: none -> 96.9 us  [swap_groups(): lax.all_to_all(blocks, 'seq', split_axis=0, concat_axis=0, tiled=True)]
    all_gather x1, waiting for transfers between devices: 0.02 us -> 57.7 us  [local(): lax.all_gather(narrow_weight, ('dp', 'seq'), axis=0, tiled=True)]
    pallas_call x0 -> x4, Pallas kernels: none -> 54.1 us  [the longest x2 30.8 us: attend_backward(): pl.pallas_call(functools.partial(attend_backward_body, n, rows), grid_spe...]
    dynamic_update_slice x72 -> x0, local copies, waits for them, and re-layouts: 51.3 us -> none  [the longest x24 25.5 us: forward_layer(): lax.map(attend_forward, (queries, key_rows, values, item_lengths))]
  transfers between devices with their start and end apart: 16 -> 12, of which waited for: 12 -> 12; matrix products, arithmetic and copies ran while one was open for 31% -> 9% of each run, Pallas kernels for 0% -> 1%
where the time goes in v1:
time: 1050 us
  waiting for transfers between devices  598 us (57%)
  blocking collectives  196 us (19%)
  matrix products  122 us (12%)
  Pallas kernels  54.1 us (5%)
  local copies, waits for them, and re-layouts  31.5 us (3%)
  starting transfers between devices  16.2 us (2%)
  between operations  15.3 us (1%)
  other arithmetic  13.8 us (1%)
    reduce_scatter x1, waiting for transfers between devices, local(): lax.psum_scatter(grad_terms[10], ('dp', 'seq'), scatter_dimension=0, tile...  142 us
    reduce_scatter x1, waiting for transfers between devices, local(): lax.psum_scatter(grad_terms[8], ('dp', 'seq'), scatter_dimension=0, tiled...  142 us
    reduce_scatter x1, waiting for transfers between devices, local(): lax.psum_scatter(grad_terms[4], ('dp', 'seq'), scatter_dimension=0, tiled...  102 us
    unnamed x2, blocking collectives  99.5 us
    all_to_all x4, blocking collectives, swap_groups(): lax.all_to_all(blocks, 'seq', split_axis=0, concat_axis=0, tiled=True)  96.9 us
    all_to_all x4, waiting for transfers between devices, swap_groups(): lax.all_to_all(blocks, 'seq', split_axis=0, concat_axis=0, tiled=True)  70.1 us
    all_gather x1, waiting for transfers between devices, local(): lax.all_gather(narrow_weight, ('dp', 'seq'), axis=0, tiled=True)  57.7 us
    all_gather x1, waiting for transfers between devices, local(): lax.all_gather(widen_weight, ('dp', 'seq'), axis=0, tiled=True)  51.1 us
  transfers between devices with their start and end apart: 12, of which 12 were waited for; matrix products, arithmetic and copies ran while one was open for 9% of the time, Pallas kernels for 1%

profile of v1, /device:TPU:0, one launch (start us, length us, event | category | flops | bytes accessed | tf_op | source)
XLA Modules:
  0.0 1047.6 jit_solution(3564479531530588288)
XLA Ops:
  18.1 42.7 %all-reduce.17 = (bf16[768]{0:T(1024)(128)(2,1)S(1)}, bf16[768]{0:T(1024)(128)(2,1)S(1)}, bf16[1536]{0:T(1024)(128)(2,1)S(1)}, bf16[768]{0:T(1024)(128)(2,1)S(1)...) all-reduce(bf16[768]{0:T(1024)(128)(2,1)S(1)} %dynamic-update-slice, ...), channel_id=1, replica_groups=mesh['dp'=8,'seq'=4] {'dp','seq'}, use_global_device_ids=true, to_apply=%add.1 | all-reduce | flops 9216 | bytes 36864
  62.8 11.4 %all-gather.5.cloned.1.call-done = bf16[768,2304]{1,0:T(8,128)(2,1)} async-done(((bf16[24,2304]{1,0:T(8,128)(2,1)}), bf16[768,2304]{1,0:T(8,128)(2,1)}) %all-gather.5.cloned.1.call-update) | async-done | bytes 3538960 | tf_op jit(solution)/shard_map/all_gather | solution.py:355
  82.5 32.8 %all_to_all.40.q_ref.k_ref.v_ref = bf16[4,3,3,64,512]{4,3,2,1,0:T(8,128)(2,1)} all-to-all(bf16[4,3,3,64,512]{4,3,2,1,0:T(8,128)(2,1)S(1)} %bitcast.123), channel_id=1, replica_groups=mesh['dp'=8,'seq'=4] {'seq'}, dimensions={0} | all-to-all | bytes 4718592 | tf_op jit(solution)/shard_map/all_to_all | solution.py:327
  115.3 11.6 %attend_forward.2 = (bf16[4,3,64,512]{3,2,1,0:T(8,128)(2,1)}, f32[2,3,4,256]{3,2,1,0:T(4,128)}) custom-call(s32[2]{0:T(128)} %len_ref.7, bf16[4,3,3,64,512]{4,3,2,1,0:T(8,128)(2,1)} %all_to_all.40.q_ref.k_ref.v_ref, bf16[4,3,3,64,512]{4,3,2,1,0:T(8,128)(2,1)} %all_to_all.40.q_ref.k_ref.v_ref, bf16[4,3,3,64,512]{4,3,2,1,0:T(8,128)(2,1)} %all_to_all.40.q_ref.k_ref.v_ref), custom_call_target="tpu_custom_call" | custom-call | flops 1006632960 | bytes 3145728 | tf_op jit(solution)/shard_map/attend_forward/pallas_call | solution.py:133
  131.1 11.3 %all-to-all-done.1 = bf16[4,3,64,512]{3,2,1,0:T(8,128)(2,1)S(1)} async-done(((bf16[4,3,64,512]{3,2,1,0:T(8,128)(2,1)}), bf16[4,3,64,512]{3,2,1,0:T(8,128)(2,1)S(1)}, u32[]{:S(2)}, u32[]{:S(2)}) %all-to-all-start.1) | async-done | bytes 786464 | tf_op jit(solution)/shard_map/all_to_all | solution.py:327
  145.2 51.1 %all-gather.9.cloned.1.call-done = bf16[768,3072]{1,0:T(8,128)(2,1)} async-done(((bf16[24,3072]{1,0:T(8,128)(2,1)}), bf16[768,3072]{1,0:T(8,128)(2,1)}) %all-gather.9.cloned.1.call-update) | async-done | bytes 4718608 | tf_op jit(solution)/shard_map/all_gather | solution.py:361
  203.3 57.7 %all-gather.11.cloned.1.call-done = bf16[3072,768]{1,0:T(8,128)(2,1)} async-done(((bf16[96,768]{1,0:T(8,128)(2,1)}), bf16[3072,768]{1,0:T(8,128)(2,1)}) %all-gather.11.cloned.1.call-update) | async-done | bytes 4718608 | tf_op jit(solution)/shard_map/all_gather | solution.py:363
  278.1 28.4 %all-to-all-done.2.q_ref.k_ref.v_ref = bf16[4,3,3,64,512]{4,3,2,1,0:T(8,128)(2,1)S(1)} async-done(((bf16[4,3,3,64,512]{4,3,2,1,0:T(8,128)(2,1)}), bf16[4,3,3,64,512]{4,3,2,1,0:T(8,128)(2,1)S(1)}, u32[]{:S(2)}, u32[]{:S(2)}) %all-to-all-start.2) | async-done | bytes 2359328 | tf_op jit(solution)/shard_map/all_to_all | solution.py:327
  308.1 11.6 %attend_forward.3 = (bf16[4,3,64,512]{3,2,1,0:T(8,128)(2,1)}, f32[2,3,4,256]{3,2,1,0:T(4,128)}) custom-call(s32[2]{0:T(128)} %len_ref.7, bf16[4,3,3,64,512]{4,3,2,1,0:T(8,128)(2,1)} %copy-done, bf16[4,3,3,64,512]{4,3,2,1,0:T(8,128)(2,1)} %copy-done, bf16[4,3,3,64,512]{4,3,2,1,0:T(8,128)(2,1)} %copy-done), custom_call_target="tpu_custom_call" | custom-call | flops 1006632960 | bytes 3145728 | tf_op jit(solution)/shard_map/attend_forward/pallas_call | solution.py:133
  325.7 10.5 %all-to-all-done.3 = bf16[4,3,64,512]{3,2,1,0:T(8,128)(2,1)} async-done(((bf16[4,3,64,512]{3,2,1,0:T(8,128)(2,1)}), bf16[4,3,64,512]{3,2,1,0:T(8,128)(2,1)}, u32[]{:S(2)}, u32[]{:S(2)}) %all-to-all-start.3) | async-done | bytes 786464 | tf_op jit(solution)/shard_map/all_to_all | solution.py:327
  360.2 15.9 %all_to_all.41.g_ref = bf16[4,3,64,512]{3,2,1,0:T(8,128)(2,1)} all-to-all(bf16[4,3,64,512]{3,2,1,0:T(8,128)(2,1)} %bitcast.127), channel_id=1, replica_groups=mesh['dp'=8,'seq'=4] {'seq'}, dimensions={0} | all-to-all | bytes 1572864 | tf_op jit(solution)/shard_map/all_to_all | solution.py:327
  376.1 15.4 %attend_backward.2 = bf16[4,3,3,64,512]{4,3,2,1,0:T(8,128)(2,1)} custom-call(s32[2]{0:T(128)} %len_ref.7, bf16[4,3,3,64,512]{4,3,2,1,0:T(8,128)(2,1)} %copy-done, bf16[4,3,3,64,512]{4,3,2,1,0:T(8,128)(2,1)} %copy-done, bf16[4,3,3,64,512]{4,3,2,1,0:T(8,128)(2,1)} %copy-done, bf16[4,3,64,512]{3,2,1,0:T(8,128)(2,1)} %all_to_all.41.g_ref, ...), custom_call_target="tpu_custom_call" | custom-call | flops 2516582400 | bytes 6291456 | tf_op jit(solution)/shard_map/attend_backward/pallas_call | solution.py:158
  391.5 33.2 %all_to_all.42 = bf16[4,3,3,64,512]{4,3,2,1,0:T(8,128)(2,1)S(1)} all-to-all(bf16[4,3,3,64,512]{4,3,2,1,0:T(8,128)(2,1)} %attend_backward.2), channel_id=1, replica_groups=mesh['dp'=8,'seq'=4] {'seq'}, dimensions={0} | all-to-all | bytes 4718592 | tf_op jit(solution)/shard_map/all_to_all | solution.py:327
  444.6 14.9 %all_to_all.43.g_ref = bf16[4,3,64,512]{3,2,1,0:T(8,128)(2,1)} all-to-all(bf16[4,3,64,512]{3,2,1,0:T(8,128)(2,1)S(1)} %bitcast.128), channel_id=1, replica_groups=mesh['dp'=8,'seq'=4] {'seq'}, dimensions={0} | all-to-all | bytes 1572864 | tf_op jit(solution)/shard_map/all_to_all | solution.py:327
  459.5 15.4 %attend_backward.3 = bf16[4,3,3,64,512]{4,3,2,1,0:T(8,128)(2,1)} custom-call(s32[2]{0:T(128)} %len_ref.7, bf16[4,3,3,64,512]{4,3,2,1,0:T(8,128)(2,1)} %all_to_all.40.q_ref.k_ref.v_ref, bf16[4,3,3,64,512]{4,3,2,1,0:T(8,128)(2,1)} %all_to_all.40.q_ref.k_ref.v_ref, bf16[4,3,3,64,512]{4,3,2,1,0:T(8,128)(2,1)} %all_to_all.40.q_ref.k_ref.v_ref, ...), custom_call_target="tpu_custom_call" | custom-call | flops 2516582400 | bytes 6291456 | tf_op jit(solution)/shard_map/attend_backward/pallas_call | solution.py:158
  487.1 19.9 %all-to-all-done.7 = bf16[4,3,3,64,512]{4,3,2,1,0:T(8,128)(2,1)S(1)} async-done(((bf16[4,3,3,64,512]{4,3,2,1,0:T(8,128)(2,1)}), bf16[4,3,3,64,512]{4,3,2,1,0:T(8,128)(2,1)S(1)}, u32[]{:S(2)}, u32[]{:S(2)}) %all-to-all-start.7) | async-done | bytes 2359328 | tf_op jit(solution)/shard_map/all_to_all | solution.py:327
  507.0 8.2 convolution_add_fusion
  537.9 10.7 %convolution_add_fusion.1 = f32[3072,768]{1,0:T(8,128)} fusion(f32[3072,768]{1,0:T(8,128)S(1)} %fusion.56, f32[512,768]{1,0:T(8,128)S(1)} %copy-done.6, f32[512,3072]{1,0:T(8,128)} %fusion.52, f32[3072]{0:T(1024)S(1)} %convert_element_type.165), kind=kOutput, calls=%fused_computation.23 | convolution fusion | flops 2434400256 | bytes 26750976 | tf_op jit(solution)/shard_map/tf,td->fd/dot_general | solution.py:269
  550.0 10.0 multiply_convert_fusion.3
  567.8 56.7 %all-reduce.16 = (f32[768]{0:T(1024)S(1)}, f32[768]{0:T(1024)S(1)}, f32[1536]{0:T(1024)S(1)}, f32[768]{0:T(1024)S(1)}, f32[768]{0:T(1024)S(1)}, /*index=5*/f32[7...) all-reduce(f32[768]{0:T(1024)S(1)} %add.335, ...), channel_id=14, replica_groups=mesh['dp'=8,'seq'=4] {'dp','seq'}, use_global_device_ids=true, to_apply=%region_17.0.clone | all-reduce | flops 9216 | bytes 73728
  632.7 20.1 %reduce-scatter.5.cloned.1.call-done = f32[24,2304]{1,0:T(8,128)} async-done(((f32[768,2304]{1,0:T(8,128)}), f32[24,2304]{1,0:T(8,128)}) %reduce-scatter.5.cloned.1.call-update) | async-done | bytes 221200 | tf_op jit(solution)/shard_map/reduce_scatter | solution.py:414
  655.0 102.1 %reduce-scatter.7.cloned.1.call-done = f32[24,768]{1,0:T(8,128)} async-done(((f32[768,768]{1,0:T(8,128)}), f32[24,768]{1,0:T(8,128)}) %reduce-scatter.7.cloned.1.call-update) | async-done | bytes 73744 | tf_op jit(solution)/shard_map/reduce_scatter | solution.py:416
  757.0 141.6 %reduce-scatter.9.cloned.1.call-done = f32[24,3072]{1,0:T(8,128)} async-done(((f32[768,3072]{1,0:T(8,128)}), f32[24,3072]{1,0:T(8,128)}) %reduce-scatter.9.cloned.1.call-update) | async-done | bytes 294928 | tf_op jit(solution)/shard_map/reduce_scatter | solution.py:420
  898.7 141.9 %reduce-scatter.11.cloned.1.call-done = f32[96,768]{1,0:T(8,128)} async-done(((f32[3072,768]{1,0:T(8,128)}), f32[96,768]{1,0:T(8,128)}) %reduce-scatter.11.cloned.1.call-update) | async-done | bytes 294928 | tf_op jit(solution)/shard_map/reduce_scatter | solution.py:422
  (250 shorter events, 156.9 us)
Async XLA Ops:
  7.2 53.7 %copy-start.1 = (bf16[2,256,768]{2,1,0:T(8,128)(2,1)S(1)}, bf16[2,256,768]{2,1,0:T(8,128)(2,1)}, u32[]{:S(2)}) copy-start(bf16[2,256,768]{2,1,0:T(8,128)(2,1)} %param.15) | copy-start | bytes 2359300
  7.2 67.1 %all-gather.5.cloned.1.call-start = ((), (), s32[]{:S(2)}) async-start(), calls=%async_computation.12 | async-start | bytes 3649536 | tf_op jit(solution)/shard_map/all_gather | solution.py:355
  9.3 121.8 %all-gather.7.cloned.1.call-start = ((), (), s32[]{:S(2)}) async-start(), calls=%async_computation.13 | async-start | bytes 1216512 | tf_op jit(solution)/shard_map/all_gather | solution.py:357
  10.1 186.2 %all-gather.9.cloned.1.call-start = ((), (), s32[]{:S(2)}) async-start(), calls=%async_computation.14 | async-start | bytes 4866048 | tf_op jit(solution)/shard_map/all_gather | solution.py:361
  10.8 250.2 %all-gather.11.cloned.1.call-start = ((), (), s32[]{:S(2)}) async-start(), calls=%async_computation.15 | async-start | bytes 4866048 | tf_op jit(solution)/shard_map/all_gather | solution.py:363
  62.0 17.7 %copy-start.26 = (f32[512]{0:T(512)}, f32[512]{0:T(512)S(1)}, u32[]{:S(2)}) copy-start(f32[512]{0:T(512)S(1)} %rsqrt.47) | copy-start | bytes 6148
  62.0 17.7 %copy-start.28 = (f32[1,2,2,128]{3,1,2,0:T(2,128)}, f32[1,2,2,128]{3,1,2,0:T(2,128)S(1)}, u32[]{:S(2)}) copy-start(f32[1,2,2,128]{3,1,2,0:T(2,128)S(1)} %copy.57) | copy-start | bytes 6148
  127.0 15.4 %all-to-all-start.1 = ((bf16[4,3,64,512]{3,2,1,0:T(8,128)(2,1)}), bf16[4,3,64,512]{3,2,1,0:T(8,128)(2,1)S(1)}, u32[]{:S(2)}, u32[]{:S(2)}) async-start(bf16[4,3,64,512]{3,2,1,0:T(8,128)(2,1)} %get-tuple-element.18.o_ref), calls=%async_computation.1 | async-start | bytes 1572864 | tf_op jit(solution)/shard_map/all_to_all | solution.py:327
  144.8 116.2 %copy-start.2 = (f32[512,768]{1,0:T(8,128)}, f32[512,768]{1,0:T(8,128)S(1)}, u32[]{:S(2)}) copy-start(f32[512,768]{1,0:T(8,128)S(1)} %get-tuple-element.78) | copy-start | bytes 4718596
  274.5 32.1 %all-to-all-start.2 = ((bf16[4,3,3,64,512]{4,3,2,1,0:T(8,128)(2,1)}), bf16[4,3,3,64,512]{4,3,2,1,0:T(8,128)(2,1)S(1)}, u32[]{:S(2)}, u32[]{:S(2)}) async-start(bf16[4,3,3,64,512]{4,3,2,1,0:T(8,128)(2,1)} %bitcast.122), calls=%async_computation.2 | async-start | bytes 4718592 | tf_op jit(solution)/shard_map/all_to_all | solution.py:327
  319.7 16.5 %copy-start.14 = (f32[512,768]{1,0:T(8,128)S(1)}, f32[512,768]{1,0:T(8,128)}, u32[]{:S(2)}) copy-start(f32[512,768]{1,0:T(8,128)} %copy-done.13) | copy-start | bytes 4718596
  319.7 16.5 %all-to-all-start.3 = ((bf16[4,3,64,512]{3,2,1,0:T(8,128)(2,1)}), bf16[4,3,64,512]{3,2,1,0:T(8,128)(2,1)}, u32[]{:S(2)}, u32[]{:S(2)}) async-start(bf16[4,3,64,512]{3,2,1,0:T(8,128)(2,1)} %get-tuple-element.19.o_ref), calls=%async_computation.3 | async-start | bytes 1572864 | tf_op jit(solution)/shard_map/all_to_all | solution.py:327
  338.7 15.6 %copy-start.12 = (f32[512,768]{1,0:T(8,128)}, f32[512,768]{1,0:T(8,128)S(1)}, u32[]{:S(2)}) copy-start(f32[512,768]{1,0:T(8,128)S(1)} %get-tuple-element.82) | copy-start | bytes 4718596
  339.0 12.2 %slice-start.4 = ((s8[4718592]{0:T(1024)(128)(4,1)}), s8[4194304]{0:T(1024)(128)(4,1)S(1)}, s32[]{:S(2)}) async-start(s8[4718592]{0:T(1024)(128)(4,1)} %bitcast.148), calls=%async_computation.24 | async-start | bytes 8388608
  391.4 33.2 %copy-start.15 = (f32[512,768]{1,0:T(8,128)S(1)}, f32[512,768]{1,0:T(8,128)}, u32[]{:S(2)}) copy-start(f32[512,768]{1,0:T(8,128)} %copy-done.13) | copy-start | bytes 4718596
  391.4 39.7 %slice-start.2 = ((s8[4718592]{0:T(1024)(128)(4,1)}), s8[4194304]{0:T(1024)(128)(4,1)S(1)}, s32[]{:S(2)}) async-start(s8[4718592]{0:T(1024)(128)(4,1)} %bitcast.146), calls=%async_computation.22 | async-start | bytes 8388608
  391.4 39.7 %slice-start.8 = ((s8[6291456]{0:T(1024)(128)(4,1)}), s8[4194304]{0:T(1024)(128)(4,1)S(1)}, s32[]{:S(2)}) async-start(s8[6291456]{0:T(1024)(128)(4,1)} %bitcast.153), calls=%async_computation.28 | async-start | bytes 8388608
  431.1 10.4 copy-start.5
  474.9 32.1 %all-to-all-start.7 = ((bf16[4,3,3,64,512]{4,3,2,1,0:T(8,128)(2,1)}), bf16[4,3,3,64,512]{4,3,2,1,0:T(8,128)(2,1)S(1)}, u32[]{:S(2)}, u32[]{:S(2)}) async-start(bf16[4,3,3,64,512]{4,3,2,1,0:T(8,128)(2,1)} %attend_backward.3), calls=%async_computation.7 | async-start | bytes 4718592 | tf_op jit(solution)/shard_map/all_to_all | solution.py:327
  478.6 174.2 %reduce-scatter.5.cloned.1.call-start = ((), (), s32[]{:S(2)}) async-start(), calls=%async_computation.16 | async-start | bytes 7299072 | tf_op jit(solution)/shard_map/reduce_scatter | solution.py:414
  515.3 241.8 %reduce-scatter.7.cloned.1.call-start = ((), (), s32[]{:S(2)}) async-start(), calls=%async_computation.17 | async-start | bytes 2433024 | tf_op jit(solution)/shard_map/reduce_scatter | solution.py:416
  519.8 378.9 %reduce-scatter.9.cloned.1.call-start = ((), (), s32[]{:S(2)}) async-start(), calls=%async_computation.18 | async-start | bytes 9732096 | tf_op jit(solution)/shard_map/reduce_scatter | solution.py:420
  531.2 509.4 %reduce-scatter.11.cloned.1.call-start = ((), (), s32[]{:S(2)}) async-start(), calls=%async_computation.19 | async-start | bytes 9732096 | tf_op jit(solution)/shard_map/reduce_scatter | solution.py:422
  565.8 63.4 %copy-start.7 = (f32[512,768]{1,0:T(8,128)S(1)}, f32[512,768]{1,0:T(8,128)}, u32[]{:S(2)}) copy-start(f32[512,768]{1,0:T(8,128)} %copy-done.5) | copy-start | bytes 4718596
  (36 other events, 151.3 us)
Sparse Core Ops, SparseCore 0:
  11.5 62.7 all-gather.4
  77.2 53.8 all-gather.6
  134.0 62.2 all-gather.8
  199.1 61.9 all-gather.10
  515.4 137.3 reduce-scatter.4
  658.5 98.5 reduce-scatter.6
  763.5 135.1 reduce-scatter.8
  905.1 135.3 reduce-scatter.10
